TPU v7x, 256 devices: a whole 4x4x8 slice. The times are simulated.
256 devices in a mesh: ctx: 32 (over x_hi, z, core), tp: 8 (over x_lo, y).
Axes of the slice: x: 4 (x_hi: 2, x_lo: 2; x = x_hi * 2 + x_lo), y: 4, z: 8, core: 2. Of those that a mesh axis runs over, the one named last changes fastest.
Arguments:
- features: bfloat16 [3, 4096, 8192], P(None, 'ctx', 'tp'), may hold values from -6 to 6
- conv_weight: float32 [3, 3, 8192], replicated, may hold values from -3 to 3
- decay_rates: float32 [16, 8192], P(None, ('tp', 'ctx')), may hold values from 1e-05 to 0.03
- residues: float32 [16, 8192], P(None, ('tp', 'ctx')), may hold values from -1.5 to 1.5
- skip_gain: float32 [8192], P(('tp', 'ctx')), may hold values from -1 to 1
- out_weight: bfloat16 [8192, 8192], P('tp', 'ctx'), may hold values from -0.0625 to 0.0625
Outputs:
- mixed: bfloat16 [4096, 8192], P('ctx', 'tp')
All inputs are finite; a program needn't handle non-finite values.
Results may differ from a plain program's by a relative error of at most 0.014.
Values may be sent and summed in bfloat16 or wider, within the bound.
A program may use at most 64 MiB of HBM per device.

v0:
```python
import math
import jax
import jax.numpy as jnp
from jax import lax
from jax.sharding import PartitionSpec as P


def shifted(shard, axis, by):
    count = lax.axis_size(axis)
    pairs = [(i, i + by) for i in range(count) if 0 <= i + by < count]
    return lax.ppermute(shard, axis, pairs)


def angle_table(first, second, modulus):
    left = jnp.arange(first, dtype=jnp.int32)[:, None]
    right = jnp.arange(second, dtype=jnp.int32)[None, :]
    return (left * right % modulus).astype(jnp.float32) * (2.0 * math.pi / modulus)


def grid_sizes(length):
    total = 2 * length
    rows = math.gcd(total, 128)
    return (total, rows, total // rows)


def forward_dft(signal):
    count, length = signal.shape
    total, rows, cols = grid_sizes(length)
    half = rows // 2
    exact = lax.Precision.HIGH
    grid = signal.reshape(count, half, cols)
    first = angle_table(half, rows, rows)
    part_re = jnp.einsum("cab,ak->cbk", grid, jnp.cos(first), precision=exact)
    part_im = -jnp.einsum("cab,ak->cbk", grid, jnp.sin(first), precision=exact)
    twist = angle_table(cols, rows, total)
    twist_cos = jnp.cos(twist)
    twist_sin = jnp.sin(twist)
    turned_re = part_re * twist_cos + part_im * twist_sin
    turned_im = part_im * twist_cos - part_re * twist_sin
    second = angle_table(cols, cols, cols)
    second_cos = jnp.cos(second)
    second_sin = jnp.sin(second)
    out_re = jnp.einsum("cbk,bj->ckj", turned_re, second_cos, precision=exact) + jnp.einsum(
        "cbk,bj->ckj", turned_im, second_sin, precision=exact
    )
    out_im = jnp.einsum("cbk,bj->ckj", turned_im, second_cos, precision=exact) - jnp.einsum(
        "cbk,bj->ckj", turned_re, second_sin, precision=exact
    )
    return (out_re, out_im)


def inverse_dft(spec_re, spec_im, length):
    count = spec_re.shape[0]
    total, rows, cols = grid_sizes(length)
    half = rows // 2
    exact = lax.Precision.HIGH
    third = angle_table(cols, cols, cols)
    third_cos = jnp.cos(third)
    third_sin = jnp.sin(third)
    step_re = jnp.einsum("ckj,jb->ckb", spec_re, third_cos, precision=exact) - jnp.einsum(
        "ckj,jb->ckb", spec_im, third_sin, precision=exact
    )
    step_im = jnp.einsum("ckj,jb->ckb", spec_re, third_sin, precision=exact) + jnp.einsum(
        "ckj,jb->ckb", spec_im, third_cos, precision=exact
    )
    twist = angle_table(rows, cols, total)
    twist_cos = jnp.cos(twist)
    twist_sin = jnp.sin(twist)
    turned_re = step_re * twist_cos - step_im * twist_sin
    turned_im = step_re * twist_sin + step_im * twist_cos
    last = angle_table(rows, half, rows)
    result = jnp.einsum("ckb,ka->cab", turned_re, jnp.cos(last), precision=exact) - jnp.einsum(
        "ckb,ka->cab", turned_im, jnp.sin(last), precision=exact
    )
    return result.reshape(count, half * cols) / total


def long_filter(rates_local, residues_local, length):
    steps_axis = jnp.arange(length, dtype=jnp.float32)

    def add_mode(mode_index, total):
        rate_now = rates_local[mode_index][:, None]
        weight_now = residues_local[mode_index][:, None]
        return total + weight_now * jnp.sqrt(2.0 * rate_now) * jnp.exp(-rate_now * steps_axis)

    start = jnp.zeros((rates_local.shape[1], length), jnp.float32)
    return lax.fori_loop(0, rates_local.shape[0], add_mode, start)


def per_device(features, conv_weight, decay_rates, residues, skip_gain, out_weight):
    tok_rows = features.shape[1]
    width_local = features.shape[2]
    last_rows = features[:, tok_rows - 2 :, :]
    previous = shifted(last_rows, "ctx", 1)
    extended = jnp.concatenate([previous, features], axis=1).astype(jnp.float32)
    taps = conv_weight[:, :, :, None].transpose(0, 1, 3, 2)
    tp_start = lax.axis_index("tp") * width_local
    taps = lax.dynamic_slice_in_dim(taps, tp_start, width_local, 3)
    filtered = (
        taps[:, 0] * extended[:, 2:]
        + taps[:, 1] * extended[:, 1:-1]
        + taps[:, 2] * extended[:, :-2]
    )
    gate_in = (filtered[1] * filtered[2]).astype(jnp.bfloat16)
    by_channel = lax.all_to_all(gate_in.T, "ctx", split_axis=0, concat_axis=1, tiled=True)
    length = by_channel.shape[1]
    signal = by_channel.astype(jnp.float32)
    kernel = long_filter(decay_rates, residues, length)
    sig_re, sig_im = forward_dft(signal)
    ker_re, ker_im = forward_dft(kernel)
    prod_re = sig_re * ker_re - sig_im * ker_im
    prod_im = sig_re * ker_im + sig_im * ker_re
    convolved = inverse_dft(prod_re, prod_im, length)
    long_out = (convolved + skip_gain[:, None] * signal).astype(jnp.bfloat16)
    returned = lax.all_to_all(long_out, "ctx", split_axis=1, concat_axis=0, tiled=True)
    gated = (filtered[0] * returned.T.astype(jnp.float32)).astype(jnp.bfloat16)
    partial_sum = (
        jnp.dot(
            gated,
            lax.all_gather(out_weight, "ctx", axis=1, tiled=True),
            preferred_element_type=jnp.float32,
        )
        .astype(jnp.bfloat16)
        .astype(jnp.float32)
    )
    summed = lax.psum(partial_sum.astype(jnp.bfloat16), "tp").astype(jnp.float32)
    kept = lax.dynamic_slice_in_dim(summed, tp_start, width_local, 1)
    return kept.astype(jnp.bfloat16)


def solution(mesh):
    in_specs = (
        P(None, "ctx", "tp"),
        P(),
        P(None, ("tp", "ctx")),
        P(None, ("tp", "ctx")),
        P(("tp", "ctx")),
        P("tp", "ctx"),
    )
    out_specs = P("ctx", "tp")
    return jax.shard_map(
        per_device, mesh=mesh, in_specs=in_specs, out_specs=out_specs, check_vma=False
    )
```

profile of v0, /device:TPU:4, one launch (start us, length us, event | category | flops | bytes accessed | tf_op | source)
XLA Modules:
  0.0 274.4 jit_solution(14337545069532780381)
XLA Ops:
  7.3 1.4 slice.31
  8.7 1.9 collective-permute-start
  10.6 15.2 %while.14 = (s32[]{:T(128)}, f32[32,4096]{1,0:T(8,128)S(1)}, f32[16,32]{1,0:T(8,128)}, f32[16,32]{1,0:T(8,128)}, s32[]{:T(128)}, /*index=5*/s32[]{:T(128)}) while((s32[]{:T(128)}, f32[32,4096]{1,0:T(8,128)S(1)}, f32[16,32]{1,0:T(8,128)}, f32[16,32]{1,0:T(8,128)}, s32[]{:T(128)}, /*index=5*/s32[]{:T(128)}) %tuple.41), condition=%wide.region_1.0_spmd.clone, body=%wide.region_0.0_spmd.clone.sunk | while | flops 524387 | bytes 1049427 | solution.py:87
  10.6 0.7 multiply_bitcast_fusion.2
  11.6 0.7 multiply_bitcast_fusion.2
  12.5 0.7 multiply_bitcast_fusion.2
  13.5 0.7 multiply_bitcast_fusion.2
  14.4 0.7 multiply_bitcast_fusion.2
  15.4 0.7 multiply_bitcast_fusion.2
  16.3 0.7 multiply_bitcast_fusion.2
  17.3 0.7 multiply_bitcast_fusion.2
  18.2 0.7 multiply_bitcast_fusion.2
  19.2 0.7 multiply_bitcast_fusion.2
  20.1 0.7 multiply_bitcast_fusion.2
  21.1 0.7 multiply_bitcast_fusion.2
  23.0 0.7 multiply_bitcast_fusion.2
  23.9 0.7 multiply_bitcast_fusion.2
  24.9 0.7 multiply_bitcast_fusion.2
  27.1 1.0 convolution_negate_fusion.1
  28.1 1.0 fusion.56
  29.1 0.7 fusion.27
  29.9 0.8 convolution_subtract_fusion.2
  31.2 2.3 copy.28
  33.5 1.3 copy.48
  34.8 2.0 copy.27
  36.8 2.0 maximum_convert_fusion
  38.8 2.4 fusion.5
  41.2 1.2 copy-done.1
  42.4 0.8 fusion.16
  43.1 12.4 %all-to-all-start = ((bf16[32,32,128]{2,1,0:T(8,128)(2,1)}), bf16[32,32,128]{2,1,0:T(8,128)(2,1)}, u32[]{:S(2)}, u32[]{:S(2)}) async-start(bf16[32,32,128]{2,1,0:T(8,128)(2,1)} %bitcast.90), calls=%async_computation | async-start | bytes 524288 | tf_op jit(solution)/shard_map/all_to_all | solution.py:105
  55.8 1.6 fusion.26
  57.4 0.8 fusion.102
  58.1 1.7 convolution_add_fusion.1
  59.9 8.3 %all-to-all-done = bf16[32,32,128]{2,1,0:T(8,128)(2,1)} async-done(((bf16[32,32,128]{2,1,0:T(8,128)(2,1)}), bf16[32,32,128]{2,1,0:T(8,128)(2,1)}, u32[]{:S(2)}, u32[]{:S(2)}) %all-to-all-start) | async-done | bytes 262176 | tf_op jit(solution)/shard_map/all_to_all | solution.py:105
  68.2 1.1 copy.29
  70.7 0.7 fusion.25
  71.5 0.7 fusion.24
  72.2 0.8 convolution_add_fusion.2
  73.5 1.1 multiply_add_fusion
  77.5 1.7 fusion.12
  79.2 1.7 fusion.8
  81.6 1.5 fusion.19
  83.1 20.5 %all_to_all.26 = bf16[32,32,128]{2,0,1:T(8,128)(2,1)S(1)} all-to-all(bf16[32,32,128]{2,0,1:T(8,128)(2,1)S(1)} %fusion.19), channel_id=1, replica_groups=mesh['ctx'=32,'tp'=8] {'ctx'}, dimensions={1} | all-to-all | bytes 524288 | tf_op jit(solution)/shard_map/all_to_all | solution.py:115
  103.6 1.1 fusion.18
  104.7 66.7 %all-gather.2.cloned.1.call-done = bf16[1024,8192]{1,0:T(8,128)(2,1)} async-done(((bf16[1024,256]{1,0:T(8,128)(2,1)}), bf16[1024,8192]{1,0:T(8,128)(2,1)}) %all-gather.2.cloned.1.call-update) | async-done | bytes 16777232 | tf_op jit(solution)/shard_map/all_gather | solution.py:120
  171.4 9.6 %convolution_convert_fusion = bf16[128,8192]{1,0:T(8,128)(2,1)} fusion(bf16[128,1024]{0,1:T(8,128)(2,1)S(1)} %fusion.18, bf16[1024,8192]{1,0:T(8,128)(2,1)} %all-gather.2.cloned.1.call-done), kind=kOutput, calls=%fused_computation.8 | convolution fusion | flops 2148532224 | bytes 19136512 | tf_op jit(solution)/shard_map/dot_general | solution.py:118
  181.0 84.9 %all-reduce.2.cloned.1.call-done = bf16[128,8192]{1,0:T(8,128)(2,1)} async-done(((bf16[128,8192]{1,0:T(8,128)(2,1)}), bf16[128,8192]{1,0:T(8,128)(2,1)}) %all-reduce.2.cloned.1.call-update) | async-done | bytes 2097168 | tf_op jit(solution)/shard_map/psum | solution.py:126
  265.9 1.7 convert_convert_fusion
  (63 shorter events, 12.2 us)
Async XLA Ops:
  6.5 19.7 %copy-start = (f32[3,3,8192]{2,1,0:T(4,128)S(1)}, f32[3,3,8192]{2,1,0:T(4,128)}, u32[]{:S(2)}) copy-start(f32[3,3,8192]{2,1,0:T(4,128)} %param.9) | copy-start | bytes 884740
  6.5 164.9 %all-gather.2.cloned.1.call-start = ((), (), s32[]{:S(2)}) async-start(), calls=%async_computation.2 | async-start | bytes 17301504 | tf_op jit(solution)/shard_map/all_gather | solution.py:120
  8.7 26.2 %collective-permute-start = (bf16[3,2,1024]{2,1,0:T(2,128)(2,1)}, bf16[3,2,1024]{2,1,0:T(2,128)(2,1)}, u32[]{:S(2)}, u32[]{:S(2)}) collective-permute-start(bf16[3,2,1024]{2,1,0:T(2,128)(2,1)} %slice.31), channel_id=1, source_target_pairs={{0,8},{8,16},{16,24},{24,32},{32,40},{40,48},{48,56},{56,64},{64,7... | collective-permute-start | bytes 36872 | tf_op jit(solution)/shard_map/ppermute | solution.py:11
  26.4 3.4 %copy-start.6 = (f32[64,128]{1,0:T(8,128)}, f32[64,128]{1,0:T(8,128)S(1)}, u32[]{:S(2)}) copy-start(f32[64,128]{1,0:T(8,128)S(1)} %get-tuple-element.135) | copy-start | bytes 98308
  26.4 4.2 %copy-start.3 = (f32[64,128]{1,0:T(8,128)}, f32[64,128]{1,0:T(8,128)S(1)}, u32[]{:S(2)}) copy-start(f32[64,128]{1,0:T(8,128)S(1)} %get-tuple-element.134) | copy-start | bytes 98308
  36.8 2.0 copy-start.11
  36.8 2.0 copy-start.12
  41.2 1.2 copy-start.1
  43.1 25.0 %all-to-all-start = ((bf16[32,32,128]{2,1,0:T(8,128)(2,1)}), bf16[32,32,128]{2,1,0:T(8,128)(2,1)}, u32[]{:S(2)}, u32[]{:S(2)}) async-start(bf16[32,32,128]{2,1,0:T(8,128)(2,1)} %bitcast.90), calls=%async_computation | async-start | bytes 524288 | tf_op jit(solution)/shard_map/all_to_all | solution.py:105
  55.5 210.4 %all-reduce.2.cloned.1.call-start = ((), (), s32[]{:S(2)}) async-start(), calls=%async_computation.3 | async-start | bytes 4194304 | tf_op jit(solution)/shard_map/psum | solution.py:126
  55.8 2.4 copy-start.4
  55.8 2.4 copy-start.7
  69.5 1.2 copy-start.5
  69.5 1.2 copy-start.8
  72.2 1.2 copy-start.2
  76.7 0.8 copy-start.9
  76.7 0.8 copy-start.10
  80.9 0.7 copy-start.13
Sparse Core Ops, SparseCore 0:
  9.9 161.4 all-gather.1
  181.1 84.7 all-reduce.1
where the time goes:
time: 276 us; the launch traced here: 274 us
  waiting for transfers between devices  161 us (58%)
  matrix products  27.2 us (10%)
  other arithmetic  25.1 us (9%)
  blocking collectives  20.5 us (7%)
  starting transfers between devices  14.5 us (5%)
  between operations  13.8 us (5%)
  local copies, waits for them, and re-layouts  12.3 us (4%)
    psum x1, waiting for transfers between devices, per_device(): lax.psum(partial_sum.astype(jnp.bfloat16), 'tp').astype(jnp.float32)  84.9 us
    all_gather x1, waiting for transfers between devices, per_device(): lax.all_gather(out_weight, 'ctx', axis=1, tiled=True)  66.7 us
    all_to_all x1, blocking collectives, per_device(): lax.all_to_all(long_out, 'ctx', split_axis=1, concat_axis=0, tiled=True)  20.5 us
    all_to_all x1, starting transfers between devices, per_device(): lax.all_to_all(gate_in.T, 'ctx', split_axis=0, concat_axis=1, tiled=True)  12.4 us
    mul x16, other arithmetic, add_mode(): weight_now * jnp.sqrt(2.0 * rate_now) * jnp.exp(-rate_now * steps_axis)  11.5 us
    dot_general x1, matrix products, per_device(): jnp.dot(gated, lax.all_gather(out_weight, 'ctx', axis=1, tiled=True), pre...  9.56 us
    all_to_all x1, waiting for transfers between devices, per_device(): lax.all_to_all(gate_in.T, 'ctx', split_axis=0, concat_axis=1, tiled=True)  8.31 us
    unnamed x31, local copies, waits for them, and re-layouts  6.34 us
  transfers between devices with their start and end apart: 4, of which 3 were waited for; matrix products, arithmetic and copies ran while one was open for 19% of the time, Pallas kernels for 0%

commit v1 on v0

--- a/solution.py
+++ b/solution.py
@@ -3,6 +3,7 @@
 import jax.numpy as jnp
 from jax import lax
 from jax.sharding import PartitionSpec as P
+from jax.lax import all_to_all, axis_size
 
 
 def shifted(shard, axis, by):
@@ -114,12 +115,12 @@
     long_out = (convolved + skip_gain[:, None] * signal).astype(jnp.bfloat16)
     returned = lax.all_to_all(long_out, "ctx", split_axis=1, concat_axis=0, tiled=True)
     gated = (filtered[0] * returned.T.astype(jnp.float32)).astype(jnp.bfloat16)
+    _rest_seats_all = lambda sample: jnp.concatenate(
+        all_to_all(jnp.stack([sample] * axis_size("ctx")), "ctx", split_axis=0, concat_axis=0),
+        axis=1,
+    )
     partial_sum = (
-        jnp.dot(
-            gated,
-            lax.all_gather(out_weight, "ctx", axis=1, tiled=True),
-            preferred_element_type=jnp.float32,
-        )
+        jnp.dot(gated, _rest_seats_all(out_weight), preferred_element_type=jnp.float32)
         .astype(jnp.bfloat16)
         .astype(jnp.float32)
     )

time: 276 us -> 593 us (2.15)
  waiting for transfers between devices: 161 us -> 478 us
  blocking collectives: 20.5 us -> 0 us
  starting transfers between devices: 14.5 us -> 29.2 us
    all_to_all x0 -> x2, waiting for transfers between devices: none -> 379 us  [the longest x1 368 us: per_device(): all_to_all(jnp.stack([sample] * axis_size('ctx')), 'ctx', split_axis=0, c...]
    all_gather x1 -> x0, waiting for transfers between devices: 66.7 us -> none  [per_device(): lax.all_gather(out_weight, 'ctx', axis=1, tiled=True)]
    all_to_all x1 -> x0, blocking collectives: 20.5 us -> none  [per_device(): lax.all_to_all(long_out, 'ctx', split_axis=1, concat_axis=0, tiled=True)]
    all_to_all x0 -> x2, starting transfers between devices: none -> 14.8 us  [the longest x1 8.05 us: per_device(): all_to_all(jnp.stack([sample] * axis_size('ctx')), 'ctx', split_axis=0, c...]
    another operation x0 -> x1, local copies, waits for them, and re-layouts: none -> 6.01 us  [per_device(): jnp.stack([sample] * axis_size('ctx'))]
  transfers between devices with their start and end apart: 4 -> 5, of which waited for: 3 -> 4; matrix products, arithmetic and copies ran while one was open for 19% -> 5% of each run, Pallas kernels for 0% -> 0%
where the time goes in v1:
time: 593 us; the launch traced here: 591 us
  waiting for transfers between devices  478 us (81%)
  matrix products  31.2 us (5%)
  starting transfers between devices  29.2 us (5%)
  other arithmetic  24.9 us (4%)
  local copies, waits for them, and re-layouts  14 us (2%)
  between operations  13.7 us (2%)
    all_to_all x1, waiting for transfers between devices, per_device(): all_to_all(jnp.stack([sample] * axis_size('ctx')), 'ctx', split_axis=0, c...  368 us
    psum x1, waiting for transfers between devices, per_device(): lax.psum(partial_sum.astype(jnp.bfloat16), 'tp').astype(jnp.float32)  90 us
    dot_general x1, matrix products, per_device(): jnp.dot(gated, _rest_seats_all(out_weight), preferred_element_type=jnp.fl...  12.8 us
    all_to_all x1, starting transfers between devices, per_device(): lax.all_to_all(gate_in.T, 'ctx', split_axis=0, concat_axis=1, tiled=True)  12.5 us
  transfers between devices with their start and end apart: 5, of which 4 were waited for; matrix products, arithmetic and copies ran while one was open for 5% of the time, Pallas kernels for 0%

profile of v1, /device:TPU:4, one launch (start us, length us, event | category | flops | bytes accessed | tf_op | source)
XLA Modules:
  0.0 591.4 jit_solution(10960782779868109835)
XLA Ops:
  6.5 0.9 slice.31
  7.4 1.9 collective-permute-start
  9.3 0.8 fusion.94
  10.1 15.2 %while.14 = (s32[]{:T(128)}, f32[32,4096]{1,0:T(8,128)S(1)}, f32[16,32]{1,0:T(8,128)}, f32[16,32]{1,0:T(8,128)}, s32[]{:T(128)}, /*index=5*/s32[]{:T(128)}) while((s32[]{:T(128)}, f32[32,4096]{1,0:T(8,128)S(1)}, f32[16,32]{1,0:T(8,128)}, f32[16,32]{1,0:T(8,128)}, s32[]{:T(128)}, /*index=5*/s32[]{:T(128)}) %tuple.41), condition=%wide.region_1.0_spmd.clone, body=%wide.region_0.0_spmd.clone.sunk | while | flops 524387 | bytes 1049435 | solution.py:88
  11.1 0.7 multiply_bitcast_fusion.2
  12.0 0.7 multiply_bitcast_fusion.2
  13.0 0.7 multiply_bitcast_fusion.2
  13.9 0.7 multiply_bitcast_fusion.2
  14.9 0.7 multiply_bitcast_fusion.2
  15.8 0.7 multiply_bitcast_fusion.2
  16.8 0.7 multiply_bitcast_fusion.2
  17.7 0.7 multiply_bitcast_fusion.2
  18.7 0.7 multiply_bitcast_fusion.2
  19.6 0.7 multiply_bitcast_fusion.2
  20.6 0.7 multiply_bitcast_fusion.2
  21.5 0.7 multiply_bitcast_fusion.2
  23.5 0.7 multiply_bitcast_fusion.2
  25.8 1.0 convolution_negate_fusion.1
  26.8 1.0 fusion.56
  27.9 1.5 fusion.27
  29.4 1.5 convolution_subtract_fusion.2
  30.9 2.3 copy.30
  33.3 2.0 copy.29
  35.2 2.0 maximum_convert_fusion
  37.2 2.4 fusion.5
  39.6 1.1 copy-done.2
  40.7 0.8 fusion.16
  41.5 12.5 %all-to-all-start = ((bf16[32,32,128]{2,1,0:T(8,128)(2,1)}), bf16[32,32,128]{2,1,0:T(8,128)(2,1)S(1)}, u32[]{:S(2)}, u32[]{:S(2)}) async-start(bf16[32,32,128]{2,1,0:T(8,128)(2,1)} %bitcast.94), calls=%async_computation | async-start | bytes 524288 | tf_op jit(solution)/shard_map/all_to_all | solution.py:106
  54.0 0.7 fusion.26
  54.9 1.8 convolution_add_fusion.1
  56.6 9.0 %all-to-all-done = bf16[32,32,128]{2,1,0:T(8,128)(2,1)S(1)} async-done(((bf16[32,32,128]{2,1,0:T(8,128)(2,1)}), bf16[32,32,128]{2,1,0:T(8,128)(2,1)S(1)}, u32[]{:S(2)}, u32[]{:S(2)}) %all-to-all-start) | async-done | bytes 262176 | tf_op jit(solution)/shard_map/all_to_all | solution.py:106
  67.2 0.7 fusion.25
  67.9 0.7 fusion.24
  68.7 0.7 convolution_add_fusion.2
  69.9 1.1 multiply_add_fusion
  72.4 0.8 convolution_add_fusion
  73.9 1.7 fusion.12
  75.6 1.7 fusion.8
  77.6 1.3 fusion.19
  78.8 6.7 %all-to-all-start.1 = ((bf16[32,32,128]{2,0,1:T(8,128)(2,1)}), bf16[32,32,128]{2,0,1:T(8,128)(2,1)S(1)}, u32[]{:S(2)}, u32[]{:S(2)}) async-start(bf16[32,32,128]{2,0,1:T(8,128)(2,1)} %fusion.19), calls=%async_computation.1 | async-start | bytes 524288 | tf_op jit(solution)/shard_map/all_to_all | solution.py:116
  85.8 11.5 %all-to-all-done.1 = bf16[32,32,128]{2,0,1:T(8,128)(2,1)S(1)} async-done(((bf16[32,32,128]{2,0,1:T(8,128)(2,1)}), bf16[32,32,128]{2,0,1:T(8,128)(2,1)S(1)}, u32[]{:S(2)}, u32[]{:S(2)}) %all-to-all-start.1) | async-done | bytes 262176 | tf_op jit(solution)/shard_map/all_to_all | solution.py:116
  97.3 6.0 %stack.2 = bf16[32,1024,256]{1,2,0:T(8,128)(2,1)} broadcast(bf16[1024,256]{0,1:T(8,128)(2,1)S(1)} %copy.37), dimensions={1,2} | broadcast | bytes 17301504 | tf_op jit(solution)/shard_map/stack | solution.py:119
  103.3 8.1 %all-to-all-start.2 = ((bf16[32,1024,256]{1,2,0:T(8,128)(2,1)}), bf16[32,1024,256]{1,2,0:T(8,128)(2,1)}, u32[]{:S(2)}, u32[]{:S(2)}) async-start(bf16[32,1024,256]{1,2,0:T(8,128)(2,1)} %stack.2), calls=%async_computation.2 | async-start | bytes 33554432 | tf_op jit(solution)/shard_map/all_to_all | solution.py:119
  111.4 1.1 fusion.18
  112.5 367.5 %all-to-all-done.2 = bf16[32,1024,256]{1,2,0:T(8,128)(2,1)} async-done(((bf16[32,1024,256]{1,2,0:T(8,128)(2,1)}), bf16[32,1024,256]{1,2,0:T(8,128)(2,1)}, u32[]{:S(2)}, u32[]{:S(2)}) %all-to-all-start.2) | async-done | bytes 16777248 | tf_op jit(solution)/shard_map/all_to_all | solution.py:119
  480.0 12.8 %convolution_convert_fusion = bf16[128,8192]{1,0:T(8,128)(2,1)} fusion(bf16[128,1024]{0,1:T(8,128)(2,1)S(1)} %fusion.18, bf16[1024,8192]{0,1:T(8,128)(2,1)} %bitcast.17), kind=kOutput, calls=%fused_computation.8 | convolution fusion | flops 2148532224 | bytes 19136512 | tf_op jit(solution)/shard_map/dot_general | solution.py:123
  492.9 90.0 %all-reduce.2.cloned.1.call-done = bf16[128,8192]{1,0:T(8,128)(2,1)} async-done(((bf16[128,8192]{1,0:T(8,128)(2,1)}), bf16[128,8192]{1,0:T(8,128)(2,1)}) %all-reduce.2.cloned.1.call-update) | async-done | bytes 2097168 | tf_op jit(solution)/shard_map/psum | solution.py:127
  582.9 1.7 convert_convert_fusion
  (53 shorter events, 10.7 us)
Async XLA Ops:
  6.5 21.3 %copy-start = (f32[3,3,8192]{2,1,0:T(4,128)S(1)}, f32[3,3,8192]{2,1,0:T(4,128)}, u32[]{:S(2)}) copy-start(f32[3,3,8192]{2,1,0:T(4,128)} %param.9) | copy-start | bytes 884740
  7.4 25.8 %collective-permute-start = (bf16[3,2,1024]{2,1,0:T(2,128)(2,1)S(1)}, bf16[3,2,1024]{2,1,0:T(2,128)(2,1)}, u32[]{:S(2)}, u32[]{:S(2)}) collective-permute-start(bf16[3,2,1024]{2,1,0:T(2,128)(2,1)S(1)} %slice.31), channel_id=1, source_target_pairs={{0,8},{8,16},{16,24},{24,32},{32,40},{40,48},{48,56},{56,64},{64,7... | collective-permute-start | bytes 36872 | tf_op jit(solution)/shard_map/ppermute | solution.py:12
  37.2 16.8 %copy-start.4 = (f32[64,128]{1,0:T(8,128)S(1)}, f32[64,128]{1,0:T(8,128)}, u32[]{:S(2)}) copy-start(f32[64,128]{1,0:T(8,128)} %get-tuple-element.134) | copy-start | bytes 98308
  37.2 16.8 %copy-start.5 = (f32[64,128]{1,0:T(8,128)S(1)}, f32[64,128]{1,0:T(8,128)}, u32[]{:S(2)}) copy-start(f32[64,128]{1,0:T(8,128)} %get-tuple-element.135) | copy-start | bytes 98308
  39.6 1.1 copy-start.2
  41.5 24.1 %all-to-all-start = ((bf16[32,32,128]{2,1,0:T(8,128)(2,1)}), bf16[32,32,128]{2,1,0:T(8,128)(2,1)S(1)}, u32[]{:S(2)}, u32[]{:S(2)}) async-start(bf16[32,32,128]{2,1,0:T(8,128)(2,1)} %bitcast.94), calls=%async_computation | async-start | bytes 524288 | tf_op jit(solution)/shard_map/all_to_all | solution.py:106
  68.7 1.2 copy-start.3
  75.6 1.9 copy-start.7
  77.3 8.2 %copy-start.6 = (bf16[1024,256]{1,0:T(8,128)(2,1)S(1)}, bf16[1024,256]{1,0:T(8,128)(2,1)}, u32[]{:S(2)}) copy-start(bf16[1024,256]{1,0:T(8,128)(2,1)} %param.13) | copy-start | bytes 1572868
  78.8 18.5 %all-to-all-start.1 = ((bf16[32,32,128]{2,0,1:T(8,128)(2,1)}), bf16[32,32,128]{2,0,1:T(8,128)(2,1)S(1)}, u32[]{:S(2)}, u32[]{:S(2)}) async-start(bf16[32,32,128]{2,0,1:T(8,128)(2,1)} %fusion.19), calls=%async_computation.1 | async-start | bytes 524288 | tf_op jit(solution)/shard_map/all_to_all | solution.py:116
  103.3 376.7 %all-to-all-start.2 = ((bf16[32,1024,256]{1,2,0:T(8,128)(2,1)}), bf16[32,1024,256]{1,2,0:T(8,128)(2,1)}, u32[]{:S(2)}, u32[]{:S(2)}) async-start(bf16[32,1024,256]{1,2,0:T(8,128)(2,1)} %stack.2), calls=%async_computation.2 | async-start | bytes 33554432 | tf_op jit(solution)/shard_map/all_to_all | solution.py:119
  111.4 471.5 %all-reduce.2.cloned.1.call-start = ((), (), s32[]{:S(2)}) async-start(), calls=%async_computation.3 | async-start | bytes 4194304 | tf_op jit(solution)/shard_map/psum | solution.py:127
  480.0 104.5 %copy-start.1 = (f32[3,3,8192]{2,1,0:T(4,128)S(1)}, f32[3,3,8192]{2,1,0:T(4,128)}, u32[]{:S(2)}) copy-start(f32[3,3,8192]{2,1,0:T(4,128)} %param.9) | copy-start | bytes 884740
Sparse Core Ops, SparseCore 0:
  493.0 89.8 all-reduce.1
